TPU v7x, 128 devices: a whole 4x4x4 slice. The times are simulated.
128 devices in a mesh: row: 8 (over y, core), col: 16 (over z, x).
Axes of the slice: x: 4, y: 4, z: 4, core: 2. Of those that a mesh axis runs over, the one named last changes fastest.
Arguments:
- amplitudes: float32 [96, 256, 1024], P('col', None, 'row'), may hold values from -6 to 6
- interaction: float32 [16384, 16384], P('row', 'col'), may hold values from -0.5 to 0.5, as said below
- tile_counts: int32 [16], replicated, may hold values from 2 to 6, as said below
- tile_block: int32 [96], replicated, may hold values from -1 to 63, as said below
- recouple_sign: int32 [96], replicated, may hold values from 0 to 1
- orbit_perm: int32 [96, 256], replicated, may hold values from 0 to 255, each once within a row
- particle_energy: float32 [96, 256], P('col'), may hold values from -2 to 2
Outputs:
- sigma: float32 [96, 256, 1024], P('col', None, 'row')
Inputs may be any that keep to these rules, and one draw needn't show every extreme that they name: Owner c holds its live tiles in its first tile_counts[c] slots; the counts sum to 64, and some owner holds 6. `tile_block`: live slots map one to one onto the 64 cross-channel tiles, and slots that are not live hold -1; two live tiles of one owner never lie in the same aligned group of 4 cross-channel tiles. interaction equals its transpose.
All inputs are finite; a program needn't handle non-finite values.
Results may differ from a plain program's by a relative error of at most 0.000061.
Values sent between devices are 32-bit elements; how exact they have to be, the bound alone decides.
A program may use at most 128 MiB of HBM per device.

v0:
```python
import jax
import jax.numpy as jnp
from jax import lax
from jax.sharding import PartitionSpec as P


def split_up(value, dim, length):
    before, after = (value.shape[:dim], value.shape[dim + 1 :])
    return jnp.moveaxis(value.reshape(*before, length, -1, *after), dim, 0)


def sum_at_owner(value, axis, dim):
    length = lax.axis_size(axis)
    tiles = lax.all_to_all(split_up(value, dim, length), axis, 0, 0, tiled=True)
    return jnp.sum(tiles, axis=0)


def tile_recouple(tiles, phases, orders):
    moved = jax.vmap(lambda single, ordering: jnp.take(single, ordering, axis=0))(tiles, orders)
    return moved * phases[:, None, None]


def local(
    amplitudes, interaction, tile_counts, tile_block, recouple_sign, orbit_perm, particle_energy
):
    column_index = lax.axis_index("col")
    row_index = lax.axis_index("row")
    column_count = lax.axis_size("col")
    slots, tile_rows, narrow_cols = amplitudes.shape
    row_blocks = interaction.shape[0] // tile_rows
    col_blocks = interaction.shape[1] // tile_rows
    tile_total = tile_block.shape[0]
    slot_ids = jnp.arange(slots, dtype=jnp.int32)
    is_live = slot_ids < jnp.take(tile_counts, column_index)
    live_mask = is_live.astype(jnp.float32)[:, None, None]
    own_block = jnp.where(
        is_live, lax.dynamic_slice_in_dim(tile_block, column_index * slots, slots), -1
    )
    all_phases = (1 - 2 * recouple_sign).astype(jnp.float32)
    own_phases = lax.dynamic_slice_in_dim(all_phases, column_index * slots, slots)
    own_orders = lax.dynamic_slice_in_dim(orbit_perm, column_index * slots, slots, 0)
    diagonal = particle_energy[:, :, None] * amplitudes
    tile_ids = jnp.arange(tile_total, dtype=jnp.int32)
    peer_ids = jnp.arange(column_count, dtype=jnp.int32)

    def tiles_of(blocks):
        matches = tile_block[None, :] == blocks[:, None]
        return jnp.sum(jnp.where(matches, tile_ids[None, :], 0), axis=1)

    target_col = own_block // col_blocks
    my_blocks = column_index * col_blocks + jnp.arange(col_blocks, dtype=jnp.int32)
    block_tiles = tiles_of(my_blocks)
    widened = lax.all_gather(amplitudes, "row", axis=2, tiled=True)
    widened = tile_recouple(widened, own_phases, own_orders)
    group_blocks = row_index * row_blocks + jnp.arange(row_blocks, dtype=jnp.int32)
    group_tiles = tiles_of(group_blocks)
    is_owned = group_tiles // slots == column_index
    placed = (
        jnp.take(widened, group_tiles % slots, axis=0) * is_owned.astype(jnp.float32)[:, None, None]
    )
    crossed = lax.psum(placed.reshape(row_blocks * tile_rows, widened.shape[2]), "col")
    partial_cols = lax.dot_general(
        interaction,
        crossed,
        (((0,), (0,)), ((), ())),
        precision=lax.Precision.HIGHEST,
        preferred_element_type=jnp.float32,
    )
    own_part = sum_at_owner(partial_cols, "row", 1)
    blocks_here = own_part.reshape(col_blocks, tile_rows, narrow_cols)
    block_inverse = jnp.argsort(jnp.take(orbit_perm, block_tiles, axis=0), axis=1)
    blocks_here = tile_recouple(blocks_here, jnp.take(all_phases, block_tiles), block_inverse)
    block_owner = block_tiles // slots
    choose_mask = block_owner[None, :] == peer_ids[:, None]
    choose_block = jnp.sum(
        jnp.where(choose_mask, jnp.arange(col_blocks, dtype=jnp.int32)[None, :], 0), axis=1
    )
    choose_weight = jnp.max(choose_mask.astype(jnp.float32), axis=1)
    outgoing = jnp.take(blocks_here, choose_block, axis=0) * choose_weight[:, None, None]
    arrived = lax.all_to_all(outgoing, "col", split_axis=0, concat_axis=0, tiled=True)
    returned = jnp.take(arrived, jnp.clip(target_col, 0, column_count - 1), axis=0)
    return (returned + diagonal) * live_mask


def solution(mesh):
    placed = (P("col", None, "row"), P("row", "col"), P(), P(), P(), P(), P("col", None))
    return jax.shard_map(
        local, mesh=mesh, in_specs=placed, out_specs=P("col", None, "row"), check_vma=False
    )
```

profile of v0, /device:TPU:0, one launch (start us, length us, event | category | flops | bytes accessed | tf_op | source)
XLA Modules:
  0.0 393.0 jit_solution(7255663869322990882)
XLA Ops:
  7.4 0.7 all-gather.2.cloned.1.call-update
  8.1 0.7 subtract_convert_fusion
  8.9 0.7 bitcast_or_fusion
  9.6 0.8 select_reduce_fusion
  10.7 0.7 compare_and_fusion
  11.4 45.4 %all-gather.2.cloned.1.call-done = f32[6,256,1024]{2,1,0:T(8,128)} async-done(((f32[6,256,128]{2,1,0:T(8,128)}), f32[6,256,1024]{2,1,0:T(8,128)}) %all-gather.2.cloned.1.call-update) | async-done | bytes 6291472 | tf_op jit(solution)/shard_map/all_gather | solution.py:53
  56.8 30.5 %gather_fusion.5 = f32[1536,1024]{1,0:T(8,128)} fusion(f32[6,256,1024]{2,1,0:T(8,128)} %all-gather.2.cloned.1.call-done, s32[1536]{0:T(1024)S(1)} %reshape.221), kind=kCustom, calls=%fused_computation.5 | custom fusion | bytes 12595200 | tf_op jit(solution)/shard_map/vmap(jit(_take))/gather | solution.py:19
  87.3 4.9 %select_multiply_fusion = f32[6,256,1024]{2,1,0:T(8,128)} fusion(f32[6,256,1024]{2,1,0:T(8,128)} %bitcast.45, f32[6]{0:T(128)S(1)} %dynamic_slice.11, pred[6,256]{1,0:T(8,128)(4,1)S(1)} %compare_and_fusion), kind=kLoop, calls=%fused_computation.9 | loop fusion | flops 3145728 | bytes 12584472 | tf_op jit(solution)/shard_map/mul | solution.py:20
  92.2 7.1 %gather_fusion.1 = f32[8,256,1024]{2,1,0:T(8,128)} fusion(f32[6,256,1024]{2,1,0:T(8,128)} %select_multiply_fusion, s32[1024]{0:T(1024)S(1)} %pad_clamp_fusion.2), kind=kCustom, calls=%fused_computation.1 | custom fusion | bytes 16777248 | tf_op jit(solution)/shard_map/jit(_take)/gather | solution.py:59
  99.3 5.8 %fusion = f32[2048,1024]{1,0:T(8,128)} fusion(f32[8,256,1024]{2,1,0:T(8,128)} %gather_fusion.1, f32[2048]{0:T(1024)S(1)} %bitcast.48, pred[2048]{0:T(1024)(128)(4,1)S(1)} %broadcast_in_dim.145), kind=kLoop, calls=%fused_computation.8 | loop fusion | flops 4194304 | bytes 16787456 | tf_op jit(solution)/shard_map/mul | solution.py:59
  105.1 142.9 %all-reduce.2.cloned.1.call-done = f32[2048,1024]{1,0:T(8,128)} async-done(((f32[2048,1024]{1,0:T(8,128)}), f32[2048,1024]{1,0:T(8,128)}) %all-reduce.2.cloned.1.call-update) | async-done | bytes 8388624 | tf_op jit(solution)/shard_map/psum | solution.py:61
  248.1 31.6 %fusion.5 = f32[1024,1024]{1,0:T(8,128)} fusion(f32[2048,1024]{1,0:T(8,128)} %all-reduce.2.cloned.1.call-done, f32[2048,1024]{1,0:T(8,128)} %param.8), kind=kOutput, calls=%fused_computation.61 | convolution fusion | flops 25769803776 | bytes 20971520 | tf_op jit(solution)/shard_map/dot_general | solution.py:62
  279.7 4.7 %all-to-all-start = ((f32[8,1024,128]{1,2,0:T(8,128)}), f32[8,1024,128]{1,2,0:T(8,128)}, u32[]{:S(2)}, u32[]{:S(2)}) async-start(f32[8,1024,128]{1,2,0:T(8,128)} %bitcast.46), calls=%async_computation | async-start | bytes 8388608 | tf_op jit(solution)/shard_map/all_to_all | solution.py:14
  284.4 0.2 sort.19.cloned.1.call-start
  284.8 0.6 gather_fusion.2
  285.5 1.5 gather_fusion
  286.9 0.7 broadcast_select_fusion
  287.6 0.6 iota.37
  288.4 2.7 sort.19.cloned.1.call-done
  291.1 0.7 fusion.1
  291.8 0.7 compare_and_fusion.1
  292.5 41.5 %all-to-all-done = f32[8,1024,128]{1,2,0:T(8,128)} async-done(((f32[8,1024,128]{1,2,0:T(8,128)}), f32[8,1024,128]{1,2,0:T(8,128)}, u32[]{:S(2)}, u32[]{:S(2)}) %all-to-all-start) | async-done | bytes 4194336 | tf_op jit(solution)/shard_map/all_to_all | solution.py:14
  334.0 2.6 reduce_sum.44
  336.8 6.8 %gather_fusion.6 = f32[1024,128]{1,0:T(8,128)S(1)} fusion(f32[4,256,128]{2,1,0:T(8,128)S(1)} %bitcast.44, s32[1024]{0:T(1024)S(1)} %bitcast.43), kind=kCustom, calls=%fused_computation.6 | custom fusion | bytes 1056768 | tf_op jit(solution)/shard_map/vmap(jit(_take))/gather | solution.py:19
  343.6 0.2 select_multiply_fusion.2
  343.9 0.7 gather_fusion.3
  344.6 1.6 select_multiply_fusion.1
  346.2 4.5 %all-to-all-start.1 = ((f32[16,256,128]{2,1,0:T(8,128)}), f32[16,256,128]{2,1,0:T(8,128)S(1)}, u32[]{:S(2)}, u32[]{:S(2)}) async-start(f32[16,256,128]{2,1,0:T(8,128)} %select_multiply_fusion.1), calls=%async_computation.1 | async-start | bytes 4194304 | tf_op jit(solution)/shard_map/all_to_all | solution.py:80
  350.8 0.6 dynamic-slice.2
  352.1 29.7 %all-to-all-done.1 = f32[16,256,128]{2,1,0:T(8,128)S(1)} async-done(((f32[16,256,128]{2,1,0:T(8,128)}), f32[16,256,128]{2,1,0:T(8,128)S(1)}, u32[]{:S(2)}, u32[]{:S(2)}) %all-to-all-start.1) | async-done | bytes 2097184 | tf_op jit(solution)/shard_map/all_to_all | solution.py:80
  381.8 1.5 gather_fusion.4
  383.2 2.3 add_multiply_fusion
  (37 shorter events, 1.1 us)
Async XLA Ops:
  7.4 49.4 %all-gather.2.cloned.1.call-start = ((), (), s32[]{:S(2)}) async-start(), calls=%async_computation.2 | async-start | bytes 7077888 | tf_op jit(solution)/shard_map/all_gather | solution.py:53
  8.1 240.0 %all-reduce.2.cloned.1.call-start = ((), (), s32[]{:S(2)}) async-start(), calls=%async_computation.3 | async-start | bytes 16777216 | tf_op jit(solution)/shard_map/psum | solution.py:61
  279.7 4.9 %copy-start.2 = (s32[96]{0:T(128)S(1)}, s32[96]{0:T(128)}, u32[]{:S(2)}) copy-start(s32[96]{0:T(128)} %param.10) | copy-start | bytes 1156
  279.7 54.3 %all-to-all-start = ((f32[8,1024,128]{1,2,0:T(8,128)}), f32[8,1024,128]{1,2,0:T(8,128)}, u32[]{:S(2)}, u32[]{:S(2)}) async-start(f32[8,1024,128]{1,2,0:T(8,128)} %bitcast.46), calls=%async_computation | async-start | bytes 8388608 | tf_op jit(solution)/shard_map/all_to_all | solution.py:14
  284.4 6.7 %sort.19.cloned.1.call-start = ((), (), s32[]{:S(2)}) async-start(), calls=%async_computation.4 | async-start | bytes 24608 | tf_op jit(solution)/shard_map/jit(argsort)/sort | solution.py:71
  343.8 6.9 %copy-start.3 = (s32[16]{0:T(128)S(1)}, s32[16]{0:T(128)}, u32[]{:S(2)}) copy-start(s32[16]{0:T(128)} %param.9) | copy-start | bytes 196
  343.9 39.4 %copy-start = (f32[6,256,128]{2,1,0:T(8,128)S(1)}, f32[6,256,128]{2,1,0:T(8,128)}, u32[]{:S(2)}) copy-start(f32[6,256,128]{2,1,0:T(8,128)} %param.7) | copy-start | bytes 2359300
  343.9 39.4 %copy-start.1 = (f32[6,256]{1,0:T(8,128)S(1)}, f32[6,256]{1,0:T(8,128)}, u32[]{:S(2)}) copy-start(f32[6,256]{1,0:T(8,128)} %param.13) | copy-start | bytes 18436
  346.2 35.5 %all-to-all-start.1 = ((f32[16,256,128]{2,1,0:T(8,128)}), f32[16,256,128]{2,1,0:T(8,128)S(1)}, u32[]{:S(2)}, u32[]{:S(2)}) async-start(f32[16,256,128]{2,1,0:T(8,128)} %select_multiply_fusion.1), calls=%async_computation.1 | async-start | bytes 4194304 | tf_op jit(solution)/shard_map/all_to_all | solution.py:80
Sparse Core Ops, SparseCore 0:
  9.8 46.9 all-gather.1
  105.3 142.7 all-reduce.1
Sparse Core Ops, SparseCore 1:
  288.3 2.5 sort.21.cloned.1.call-done
  (1 shorter events, 0.0 us)
where the time goes:
time: 394 us; the launch traced here: 393 us
  waiting for transfers between devices  260 us (66%)
  local copies, waits for them, and re-layouts  53.2 us (14%)
  matrix products  31.6 us (8%)
  other arithmetic  23.1 us (6%)
  between operations  15.6 us (4%)
  starting transfers between devices  9.24 us (2%)
    psum x1, waiting for transfers between devices, local(): lax.psum(placed.reshape(row_blocks * tile_rows, widened.shape[2]), 'col')  143 us
    all_gather x1, waiting for transfers between devices, local(): widened = lax.all_gather(amplitudes, 'row', axis=2, tiled=True)  45.4 us
    all_to_all x1, waiting for transfers between devices, sum_at_owner(): tiles = lax.all_to_all(split_up(value, dim, length), axis, 0, 0, tiled=True)  41.5 us
    gather x3, local copies, waits for them, and re-layouts, tile_recouple(): jnp.take(single, ordering, axis=0)  37.3 us
    dot_general x1, matrix products, local(): lax.dot_general(interaction, crossed, (((0,), (0,)), ((), ())), precision...  31.6 us
    all_to_all x1, waiting for transfers between devices, local(): lax.all_to_all(outgoing, 'col', split_axis=0, concat_axis=0, tiled=True)  29.7 us
  transfers between devices with their start and end apart: 4, of which 4 were waited for; matrix products, arithmetic and copies ran while one was open for 2% of the time, Pallas kernels for 0%

commit v1 on v0

--- a/solution.py
+++ b/solution.py
@@ -50,7 +50,9 @@
     target_col = own_block // col_blocks
     my_blocks = column_index * col_blocks + jnp.arange(col_blocks, dtype=jnp.int32)
     block_tiles = tiles_of(my_blocks)
-    widened = lax.all_gather(amplitudes, "row", axis=2, tiled=True)
+    widened = jnp.concatenate(
+        lax.all_to_all(jnp.stack([amplitudes] * lax.axis_size("row")), "row", 0, 0), axis=2
+    )
     widened = tile_recouple(widened, own_phases, own_orders)
     group_blocks = row_index * row_blocks + jnp.arange(row_blocks, dtype=jnp.int32)
     group_tiles = tiles_of(group_blocks)

time: 394 us -> 432 us (1.096)
  waiting for transfers between devices: 260 us -> 286 us
  local copies, waits for them, and re-layouts: 53.2 us -> 63.2 us
  starting transfers between devices: 9.24 us -> 14 us
    all_to_all x0 -> x1, waiting for transfers between devices: none -> 71.5 us  [local(): lax.all_to_all(jnp.stack([amplitudes] * lax.axis_size('row')), 'row', 0, 0)]
    all_gather x1 -> x0, waiting for transfers between devices: 45.4 us -> none  [local(): widened = lax.all_gather(amplitudes, 'row', axis=2, tiled=True)]
    reshape x0 -> x1, local copies, waits for them, and re-layouts: none -> 6.34 us  [local(): jnp.concatenate(lax.all_to_all(jnp.stack([amplitudes] * lax.axis_size('ro...]
    all_to_all x0 -> x1, starting transfers between devices: none -> 4.88 us  [local(): lax.all_to_all(jnp.stack([amplitudes] * lax.axis_size('row')), 'row', 0, 0)]
    another operation x0 -> x1, local copies, waits for them, and re-layouts: none -> 4.54 us  [local(): jnp.stack([amplitudes] * lax.axis_size('row'))]
  transfers between devices with their start and end apart: 4 -> 4, of which waited for: 4 -> 4; matrix products, arithmetic and copies ran while one was open for 2% -> 1% of each run, Pallas kernels for 0% -> 0%
where the time goes in v1:
time: 432 us; the launch traced here: 431 us
  waiting for transfers between devices  286 us (66%)
  local copies, waits for them, and re-layouts  63.2 us (15%)
  matrix products  31.6 us (7%)
  other arithmetic  20.3 us (5%)
  between operations  15.7 us (4%)
  starting transfers between devices  14 us (3%)
    psum x1, waiting for transfers between devices, local(): lax.psum(placed.reshape(row_blocks * tile_rows, widened.shape[2]), 'col')  143 us
    all_to_all x1, waiting for transfers between devices, local(): lax.all_to_all(jnp.stack([amplitudes] * lax.axis_size('row')), 'row', 0, 0)  71.5 us
    all_to_all x1, waiting for transfers between devices, sum_at_owner(): tiles = lax.all_to_all(split_up(value, dim, length), axis, 0, 0, tiled=True)  42.4 us
    gather x3, local copies, waits for them, and re-layouts, tile_recouple(): jnp.take(single, ordering, axis=0)  37.2 us
    dot_general x1, matrix products, local(): lax.dot_general(interaction, crossed, (((0,), (0,)), ((), ())), precision...  31.6 us
    all_to_all x1, waiting for transfers between devices, local(): lax.all_to_all(outgoing, 'col', split_axis=0, concat_axis=0, tiled=True)  29.7 us
  transfers between devices with their start and end apart: 4, of which 4 were waited for; matrix products, arithmetic and copies ran while one was open for 1% of the time, Pallas kernels for 0%

profile of v1, /device:TPU:0, one launch (start us, length us, event | category | flops | bytes accessed | tf_op | source)
XLA Modules:
  0.0 430.9 jit_solution(17521381890615685139)
XLA Ops:
  7.4 4.5 %stack.2 = f32[8,6,256,128]{3,2,1,0:T(8,128)} broadcast(f32[6,256,128]{2,1,0:T(8,128)} %param.7), dimensions={1,2,3} | broadcast | bytes 7077888 | tf_op jit(solution)/shard_map/stack | solution.py:54
  11.9 4.9 %all-to-all-start = ((f32[8,6,256,128]{3,2,1,0:T(8,128)}), f32[8,6,256,128]{3,2,1,0:T(8,128)}, u32[]{:S(2)}, u32[]{:S(2)}) async-start(f32[8,6,256,128]{3,2,1,0:T(8,128)} %stack.2), calls=%async_computation | async-start | bytes 12582912 | tf_op jit(solution)/shard_map/all_to_all | solution.py:54
  17.4 71.5 %all-to-all-done = f32[8,6,256,128]{3,2,1,0:T(8,128)} async-done(((f32[8,6,256,128]{3,2,1,0:T(8,128)}), f32[8,6,256,128]{3,2,1,0:T(8,128)}, u32[]{:S(2)}, u32[]{:S(2)}) %all-to-all-start) | async-done | bytes 6291488 | tf_op jit(solution)/shard_map/all_to_all | solution.py:54
  88.9 6.3 %copy_bitcast_fusion = f32[6,256,1024]{2,1,0:T(8,128)} fusion(f32[8,6,256,128]{3,2,1,0:T(8,128)} %all-to-all-done), kind=kLoop, calls=%fused_computation.9 | loop fusion | bytes 12582912 | tf_op jit(solution)/shard_map/reshape | solution.py:53
  95.3 30.4 %gather_fusion.5 = f32[1536,1024]{1,0:T(8,128)} fusion(f32[6,256,1024]{2,1,0:T(8,128)} %copy_bitcast_fusion, s32[1536]{0:T(1024)S(1)} %reshape.231), kind=kCustom, calls=%fused_computation.5 | custom fusion | bytes 12595200 | tf_op jit(solution)/shard_map/vmap(jit(_take))/gather | solution.py:19
  125.7 4.9 %select_multiply_fusion = f32[6,256,1024]{2,1,0:T(8,128)} fusion(f32[6,256,1024]{2,1,0:T(8,128)} %bitcast.51, f32[6]{0:T(128)S(1)} %dynamic_slice.11, pred[6,256]{1,0:T(8,128)(4,1)S(1)} %compare_and_fusion), kind=kLoop, calls=%fused_computation.10 | loop fusion | flops 3145728 | bytes 12584472 | tf_op jit(solution)/shard_map/mul | solution.py:20
  130.6 7.1 %gather_fusion.1 = f32[8,256,1024]{2,1,0:T(8,128)} fusion(f32[6,256,1024]{2,1,0:T(8,128)} %select_multiply_fusion, s32[1024]{0:T(1024)S(1)} %pad_clamp_fusion.2), kind=kCustom, calls=%fused_computation.1 | custom fusion | bytes 16777248 | tf_op jit(solution)/shard_map/jit(_take)/gather | solution.py:61
  137.7 5.8 %fusion = f32[2048,1024]{1,0:T(8,128)} fusion(f32[8,256,1024]{2,1,0:T(8,128)} %gather_fusion.1, f32[2048]{0:T(1024)S(1)} %bitcast.54, pred[2048]{0:T(1024)(128)(4,1)S(1)} %broadcast_in_dim.145), kind=kLoop, calls=%fused_computation.8 | loop fusion | flops 4194304 | bytes 16787456 | tf_op jit(solution)/shard_map/mul | solution.py:61
  143.5 142.6 %all-reduce.2.cloned.1.call-done = f32[2048,1024]{1,0:T(8,128)} async-done(((f32[2048,1024]{1,0:T(8,128)}), f32[2048,1024]{1,0:T(8,128)}) %all-reduce.2.cloned.1.call-update) | async-done | bytes 8388624 | tf_op jit(solution)/shard_map/psum | solution.py:63
  286.1 31.6 %fusion.5 = f32[1024,1024]{1,0:T(8,128)} fusion(f32[2048,1024]{1,0:T(8,128)} %all-reduce.2.cloned.1.call-done, f32[2048,1024]{1,0:T(8,128)} %param.8), kind=kOutput, calls=%fused_computation.62 | convolution fusion | flops 25769803776 | bytes 20971520 | tf_op jit(solution)/shard_map/dot_general | solution.py:64
  317.7 4.5 %all-to-all-start.1 = ((f32[8,1024,128]{1,2,0:T(8,128)}), f32[8,1024,128]{1,2,0:T(8,128)}, u32[]{:S(2)}, u32[]{:S(2)}) async-start(f32[8,1024,128]{1,2,0:T(8,128)} %bitcast.52), calls=%async_computation.1 | async-start | bytes 8388608 | tf_op jit(solution)/shard_map/all_to_all | solution.py:14
  322.3 0.2 sort.19.cloned.1.call-start
  322.5 0.2 select_reduce_fusion.2
  322.7 0.6 gather_fusion.2
  323.4 0.6 gather_fusion
  323.9 0.7 broadcast_select_fusion
  324.6 0.6 iota.37
  325.4 2.7 sort.19.cloned.1.call-done
  328.1 0.7 fusion.1
  328.8 0.7 compare_and_fusion.1
  329.5 42.4 %all-to-all-done.1 = f32[8,1024,128]{1,2,0:T(8,128)} async-done(((f32[8,1024,128]{1,2,0:T(8,128)}), f32[8,1024,128]{1,2,0:T(8,128)}, u32[]{:S(2)}, u32[]{:S(2)}) %all-to-all-start.1) | async-done | bytes 4194336 | tf_op jit(solution)/shard_map/all_to_all | solution.py:14
  371.9 2.6 reduce_sum.44
  374.5 0.2 copy.11
  374.7 6.8 %gather_fusion.6 = f32[1024,128]{1,0:T(8,128)S(1)} fusion(f32[4,256,128]{2,1,0:T(8,128)S(1)} %bitcast.50, s32[1024]{0:T(1024)S(1)} %bitcast.49), kind=kCustom, calls=%fused_computation.6 | custom fusion | bytes 1056768 | tf_op jit(solution)/shard_map/vmap(jit(_take))/gather | solution.py:19
  381.5 0.2 select_multiply_fusion.2
  381.8 0.7 gather_fusion.3
  382.5 1.6 select_multiply_fusion.1
  384.1 4.5 %all-to-all-start.2 = ((f32[16,256,128]{2,1,0:T(8,128)}), f32[16,256,128]{2,1,0:T(8,128)S(1)}, u32[]{:S(2)}, u32[]{:S(2)}) async-start(f32[16,256,128]{2,1,0:T(8,128)} %select_multiply_fusion.1), calls=%async_computation.2 | async-start | bytes 4194304 | tf_op jit(solution)/shard_map/all_to_all | solution.py:82
  388.7 0.6 dynamic-slice.2
  390.0 29.7 %all-to-all-done.2 = f32[16,256,128]{2,1,0:T(8,128)S(1)} async-done(((f32[16,256,128]{2,1,0:T(8,128)}), f32[16,256,128]{2,1,0:T(8,128)S(1)}, u32[]{:S(2)}, u32[]{:S(2)}) %all-to-all-start.2) | async-done | bytes 2097184 | tf_op jit(solution)/shard_map/all_to_all | solution.py:82
  419.7 1.5 gather_fusion.4
  421.1 2.3 add_multiply_fusion
  (42 shorter events, 0.9 us)
Async XLA Ops:
  11.9 4.9 %copy-start.4 = (s32[96]{0:T(128)S(1)}, s32[96]{0:T(128)}, u32[]{:S(2)}) copy-start(s32[96]{0:T(128)} %param.11) | copy-start | bytes 1156
  11.9 5.0 %copy-start.1 = (s32[96,256]{1,0:T(8,128)S(1)}, s32[96,256]{1,0:T(8,128)}, u32[]{:S(2)}) copy-start(s32[96,256]{1,0:T(8,128)} %param.12) | copy-start | bytes 294916
  11.9 5.1 %copy-start.3 = (s32[96]{0:T(128)S(1)}, s32[96]{0:T(128)}, u32[]{:S(2)}) copy-start(s32[96]{0:T(128)} %param.10) | copy-start | bytes 1156
  11.9 77.0 %all-to-all-start = ((f32[8,6,256,128]{3,2,1,0:T(8,128)}), f32[8,6,256,128]{3,2,1,0:T(8,128)}, u32[]{:S(2)}, u32[]{:S(2)}) async-start(f32[8,6,256,128]{3,2,1,0:T(8,128)} %stack.2), calls=%async_computation | async-start | bytes 12582912 | tf_op jit(solution)/shard_map/all_to_all | solution.py:54
  16.8 269.3 %all-reduce.2.cloned.1.call-start = ((), (), s32[]{:S(2)}) async-start(), calls=%async_computation.3 | async-start | bytes 16777216 | tf_op jit(solution)/shard_map/psum | solution.py:63
  317.7 54.2 %all-to-all-start.1 = ((f32[8,1024,128]{1,2,0:T(8,128)}), f32[8,1024,128]{1,2,0:T(8,128)}, u32[]{:S(2)}, u32[]{:S(2)}) async-start(f32[8,1024,128]{1,2,0:T(8,128)} %bitcast.52), calls=%async_computation.1 | async-start | bytes 8388608 | tf_op jit(solution)/shard_map/all_to_all | solution.py:14
  322.3 5.9 %sort.19.cloned.1.call-start = ((), (), s32[]{:S(2)}) async-start(), calls=%async_computation.4 | async-start | bytes 24608 | tf_op jit(solution)/shard_map/jit(argsort)/sort | solution.py:73
  381.7 6.9 %copy-start.5 = (s32[16]{0:T(128)S(1)}, s32[16]{0:T(128)}, u32[]{:S(2)}) copy-start(s32[16]{0:T(128)} %param.9) | copy-start | bytes 196
  381.8 39.4 %copy-start = (f32[6,256,128]{2,1,0:T(8,128)S(1)}, f32[6,256,128]{2,1,0:T(8,128)}, u32[]{:S(2)}) copy-start(f32[6,256,128]{2,1,0:T(8,128)} %param.7) | copy-start | bytes 2359300
  381.8 39.4 %copy-start.2 = (f32[6,256]{1,0:T(8,128)S(1)}, f32[6,256]{1,0:T(8,128)}, u32[]{:S(2)}) copy-start(f32[6,256]{1,0:T(8,128)} %param.13) | copy-start | bytes 18436
  384.1 35.5 %all-to-all-start.2 = ((f32[16,256,128]{2,1,0:T(8,128)}), f32[16,256,128]{2,1,0:T(8,128)S(1)}, u32[]{:S(2)}, u32[]{:S(2)}) async-start(f32[16,256,128]{2,1,0:T(8,128)} %select_multiply_fusion.1), calls=%async_computation.2 | async-start | bytes 4194304 | tf_op jit(solution)/shard_map/all_to_all | solution.py:82
Sparse Core Ops, SparseCore 0:
  143.6 142.3 all-reduce.1
Sparse Core Ops, SparseCore 1:
  325.3 2.5 sort.21.cloned.1.call-done
  (1 shorter events, 0.0 us)
